TPU v7x, 256 devices: a whole 4x4x8 slice. The times are simulated.
256 devices in a mesh: ctx: 64 (over z, y, core), ch: 4 (over x).
Axes of the slice: x: 4, y: 4, z: 8, core: 2. Of those that a mesh axis runs over, the one named last changes fastest.
Arguments:
- conv_input: bfloat16 [256, 128, 8192], P('ctx', None, 'ch'), may hold values from -6 to 6
- gate_signal: bfloat16 [256, 128, 8192], P('ctx', None, 'ch'), may hold values from -6 to 6
- cotangent: bfloat16 [256, 128, 8192], P('ctx', None, 'ch'), may hold values from -6 to 6
- filters: float32 [16, 1024], replicated
- tile_owner: int32 [192], replicated, may hold values from 0 to 63, as said below
- support: int32 [192, 8], replicated, may hold values from -1 to 191, as said below
Outputs:
- gate_grad: bfloat16 [256, 128, 8192], P('ctx', None, 'ch')
- input_grad: bfloat16 [256, 128, 8192], P('ctx', None, 'ch')
- filter_grad: float32 [16, 1024], replicated
Inputs may be any that keep to these rules, and one draw needn't show every extreme that they name: tile_owner never falls from one tile to the next; every index of ctx owns from 2 to 4 tiles, some index owns 3 + 1 and some index owns 3 - 1. support[t, k] is t - k where tile t - k belongs to the document of tile t and -1 otherwise; documents are runs of whole tiles, and some document spans 8 tiles or more.
All inputs are finite; a program needn't handle non-finite values.
Results may differ from a plain program's by a relative error of at most 0.0058.
Values may be sent and summed in bfloat16 or wider, within the bound.
No kernel may reach another device: no remote copies, remote signals or barrier semaphores. Data moves between devices by JAX's collectives and lax.ppermute only.
A program may use at most 256 MiB of HBM per device.

v0:
```python
import math
import jax
import jax.numpy as jnp
from jax import lax
from jax.sharding import PartitionSpec as P

GROUP = 128
REACH = 4


def passed_along(value, axis, steps):
    count = lax.axis_size(axis)
    leading, last = (max(0, -steps), min(count, count - steps))
    return lax.ppermute(value, axis, [(source, source + steps) for source in range(leading, last)])


def filter_blocks(filters, tile_rows, maxlag):
    narrow = filters.astype(jnp.bfloat16)
    row_ids = jnp.arange(tile_rows, dtype=jnp.int32)
    lag_offsets = (
        jnp.arange(maxlag, dtype=jnp.int32)[:, None, None] * tile_rows
        + row_ids[:, None]
        - row_ids[None, :]
    )
    picked = jnp.take(narrow, jnp.clip(lag_offsets, 0, filters.shape[1] - 1), axis=1)
    return jnp.where(lag_offsets[None] >= 0, picked, jnp.zeros_like(picked))


def lag_sums(square):
    filter_count, side_length = (square.shape[0], square.shape[1])
    flipped = square[:, :, ::-1]
    padded = jnp.pad(flipped, ((0, 0), (0, 0), (0, side_length)))
    skewed = padded.reshape(filter_count, 2 * side_length * side_length)[
        :, : side_length * (2 * side_length - 1)
    ]
    return jnp.sum(skewed.reshape(filter_count, side_length, 2 * side_length - 1), axis=1)


def spread_lags(squares, lag_count):
    maxlag, filter_count, side_length = (squares.shape[0], squares.shape[1], squares.shape[2])
    accumulated = jnp.zeros((filter_count, (maxlag + 1) * side_length), jnp.float32)
    for lag_index in range(maxlag):
        start_col = lag_index * side_length
        accumulated = accumulated.at[:, start_col : start_col + 2 * side_length - 1].add(
            lag_sums(squares[lag_index])
        )
    return accumulated[:, side_length - 1 : side_length - 1 + lag_count]


def per_device(conv_input, gate_signal, cotangent, filters, tile_owner, support):
    slot_count, tile_rows, channels = conv_input.shape
    maxlag = support.shape[1]
    filter_count, lag_count = filters.shape
    group_width = GROUP
    repeats = channels // (filter_count * group_width)
    total_tiles = tile_owner.shape[0]
    devices_ctx = lax.axis_size("ctx")
    myself = lax.axis_index("ctx")
    farthest = REACH
    devices = jnp.arange(devices_ctx, dtype=jnp.int32)
    counts = jnp.sum((tile_owner[None, :] == devices[:, None]).astype(jnp.int32), axis=1)
    starts = jnp.cumsum(counts) - counts
    slot_index = jnp.arange(slot_count, dtype=jnp.int32)
    own_tiles = starts[myself] + slot_index
    own_live = slot_index < counts[myself]
    own_safe = jnp.clip(own_tiles, 0, total_tiles - 1)
    sources = support[own_safe]
    present = own_live[:, None] & (sources >= 0)
    source_safe = jnp.clip(sources, 0, total_tiles - 1)
    holder = tile_owner[source_safe]
    within = source_safe - starts[holder]
    blocks = filter_blocks(filters, tile_rows, maxlag)
    zero_tile = jnp.zeros((), jnp.bfloat16)
    gathered = [conv_input]
    for distance in range(1, farthest + 1):
        gathered.append(passed_along(conv_input, "ctx", distance))
    window = jnp.concatenate(gathered, axis=0)
    rows_at = jnp.clip((myself - holder) * slot_count + within, 0, window.shape[0] - 1)
    selected = jnp.take(window, rows_at.reshape(-1), axis=0)
    selected = selected.reshape(slot_count, maxlag, tile_rows, channels)
    selected = jnp.where(present[:, :, None, None], selected, zero_tile)
    weighted = (gate_signal.astype(jnp.float32) * cotangent.astype(jnp.float32)).astype(
        jnp.bfloat16
    )
    weighted = jnp.where(own_live[:, None, None], weighted, zero_tile)
    weighted_shaped = weighted.reshape(slot_count, tile_rows, repeats, filter_count, group_width)
    conv_out = jnp.zeros((slot_count, tile_rows, channels), jnp.float32)
    squares = []
    for lag_index in range(maxlag):
        shaped = selected[:, lag_index].reshape(
            slot_count, tile_rows, repeats, filter_count, group_width
        )
        product = jnp.einsum(
            "fij,sjrfc->sirfc", blocks[:, lag_index], shaped, preferred_element_type=jnp.float32
        )
        conv_out = conv_out + product.reshape(slot_count, tile_rows, channels)
        squares.append(
            jnp.einsum(
                "sirfc,sjrfc->fij", weighted_shaped, shaped, preferred_element_type=jnp.float32
            )
        )
    gate_grad = (cotangent.astype(jnp.float32) * conv_out).astype(jnp.bfloat16)
    norm_factor = 1.0 / math.sqrt(
        total_tiles * tile_rows * channels * lax.axis_size("ch") / filter_count
    )
    local_filters = spread_lags(jnp.stack(squares), lag_count)
    filter_grad = lax.psum(local_filters, ("ctx", "ch")) * norm_factor
    row_count = (farthest + 1) * slot_count
    partial_value = jnp.zeros((row_count, tile_rows, channels), jnp.float32)
    back_rows = jnp.clip((myself - holder) * slot_count + within, 0, row_count - 1)
    for lag_index in range(maxlag):
        adjoint_term = jnp.einsum(
            "fji,sjrfc->sirfc",
            blocks[:, lag_index],
            weighted_shaped,
            preferred_element_type=jnp.float32,
        )
        adjoint_term = jnp.where(present[:, lag_index, None, None, None, None], adjoint_term, 0.0)
        partial_value = partial_value.at[back_rows[:, lag_index]].add(
            adjoint_term.reshape(slot_count, tile_rows, channels)
        )
    adjoint = partial_value[:slot_count]
    for distance in range(1, farthest + 1):
        adjoint = adjoint + passed_along(
            partial_value[distance * slot_count : (distance + 1) * slot_count], "ctx", -distance
        )
    input_grad = adjoint.astype(jnp.bfloat16)
    return (gate_grad, input_grad, filter_grad)


def solution(mesh):
    return jax.shard_map(
        per_device,
        mesh=mesh,
        in_specs=(P("ctx", None, "ch"), P("ctx", None, "ch"), P("ctx", None, "ch"), P(), P(), P()),
        out_specs=(P("ctx", None, "ch"), P("ctx", None, "ch"), P()),
        check_vma=False,
    )
```

profile of v0, /device:TPU:1, one launch (start us, length us, event | category | flops | bytes accessed | tf_op | source)
XLA Modules:
  0.0 1289.1 jit_solution(6269767289445348876)
XLA Ops:
  32.1 454.0 %gather_fusion.4 = bf16[131072,16]{1,0:T(8,128)(2,1)} fusion(bf16[16,1024]{0,1:T(8,128)(2,1)S(1)} %copy.164, s32[131072]{0:T(1024)S(1)} %broadcast_clamp_fusion), kind=kCustom, calls=%fused_computation.4 | custom fusion | bytes 8912896 | tf_op jit(solution)/shard_map/jit(_take)/gather | solution.py:25
  486.1 29.2 %copy.166 = bf16[8,128,128,16]{2,1,3,0:T(8,128)(2,1)} copy(bf16[8,128,128,16]{3,2,1,0:T(8,128)(2,1)} %bitcast.207) | data formatting | bytes 8388608 | tf_op jit(solution)/shard_map/jit(_take)/gather | solution.py:25
  547.7 5.4 copy.186
  553.1 4.7 copy.188
  557.7 5.4 copy.189
  563.1 4.7 copy.191
  567.8 5.4 copy.192
  573.2 4.7 copy.194
  577.8 5.4 copy.195
  583.2 4.7 copy.197
  587.9 5.4 copy.198
  593.3 4.7 copy.200
  598.0 5.6 copy.201
  603.5 4.7 copy.203
  608.2 5.4 copy.204
  618.2 5.4 copy.207
  623.9 9.7 broadcast_in_dim.155
  633.6 9.0 scatter_fusion
  642.5 9.0 scatter_fusion.1
  651.6 9.0 scatter_fusion.2
  660.6 9.0 scatter_fusion.3
  669.6 8.7 scatter_fusion.4
  678.3 8.6 scatter_fusion.5
  686.9 8.3 scatter_fusion.6
  695.1 8.3 scatter_fusion.7
  703.4 12.2 fusion.52
  742.8 11.4 gather_fusion.3
  754.2 8.7 select_select_fusion
  762.9 5.9 fusion.53
  836.1 11.8 add_bitcast_fusion
  850.1 9.3 rev.24
  863.5 6.2 reshape.668
  872.1 9.3 rev.25
  885.6 6.2 reshape.670
  893.5 6.0 rev.26
  903.6 6.2 reshape.672
  913.9 5.8 rev.27
  923.8 6.2 reshape.674
  934.1 6.0 rev.28
  944.3 6.2 reshape.676
  954.6 5.8 rev.29
  964.5 6.2 reshape.678
  974.8 6.1 rev.30
  985.0 6.2 reshape.680
  995.3 5.8 rev.31
  1005.2 6.3 reshape.682
  1028.9 241.1 %all-reduce.11.cloned.1.call-done = f32[16,1024]{1,0:T(8,128)} async-done(((f32[16,1024]{1,0:T(8,128)}), f32[16,1024]{1,0:T(8,128)}) %all-reduce.11.cloned.1.call-update) | async-done | bytes 65552 | tf_op jit(solution)/shard_map/psum | solution.py:107
  1271.5 10.4 fusion.5
  (174 shorter events, 234.9 us)
Async XLA Ops:
  7.2 24.7 %copy-start.7 = (f32[16,1024]{1,0:T(8,128)S(1)}, f32[16,1024]{1,0:T(8,128)}, u32[]{:S(2)}) copy-start(f32[16,1024]{1,0:T(8,128)} %param.25) | copy-start | bytes 196612
  7.2 1262.8 %all-reduce.11.cloned.1.call-start = ((), (), s32[]{:S(2)}) async-start(), calls=%async_computation | async-start | bytes 131072 | tf_op jit(solution)/shard_map/psum | solution.py:107
  7.2 718.4 %collective-permute-start = (bf16[4,128,2048]{2,1,0:T(8,128)(2,1)}, bf16[4,128,2048]{2,1,0:T(8,128)(2,1)}, u32[]{:S(2)}, u32[]{:S(2)}) collective-permute-start(bf16[4,128,2048]{2,1,0:T(8,128)(2,1)} %param.22), channel_id=1, source_target_pairs={{0,4},{4,8},{8,12},{12,16},{16,20},{20,24},{24,28},{28,32},{32,36}... | collective-permute-start | bytes 6291464 | tf_op jit(solution)/shard_map/ppermute | solution.py:14
  11.8 718.2 %collective-permute-start.1 = (bf16[4,128,2048]{2,1,0:T(8,128)(2,1)}, bf16[4,128,2048]{2,1,0:T(8,128)(2,1)}, u32[]{:S(2)}, u32[]{:S(2)}) collective-permute-start(bf16[4,128,2048]{2,1,0:T(8,128)(2,1)} %param.22), channel_id=1, source_target_pairs={{0,8},{4,12},{8,16},{12,20},{16,24},{20,28},{24,32},{28,36},{32,40... | collective-permute-start | bytes 6291464 | tf_op jit(solution)/shard_map/ppermute | solution.py:14
  16.3 718.2 %collective-permute-start.2 = (bf16[4,128,2048]{2,1,0:T(8,128)(2,1)}, bf16[4,128,2048]{2,1,0:T(8,128)(2,1)}, u32[]{:S(2)}, u32[]{:S(2)}) collective-permute-start(bf16[4,128,2048]{2,1,0:T(8,128)(2,1)} %param.22), channel_id=1, source_target_pairs={{0,12},{4,16},{8,20},{12,24},{16,28},{20,32},{24,36},{28,40},{32,4... | collective-permute-start | bytes 6291464 | tf_op jit(solution)/shard_map/ppermute | solution.py:14
  19.9 719.7 %collective-permute-start.3 = (bf16[4,128,2048]{2,1,0:T(8,128)(2,1)}, bf16[4,128,2048]{2,1,0:T(8,128)(2,1)}, u32[]{:S(2)}, u32[]{:S(2)}) collective-permute-start(bf16[4,128,2048]{2,1,0:T(8,128)(2,1)} %param.22), channel_id=1, source_target_pairs={{0,16},{4,20},{8,24},{12,28},{16,32},{20,36},{24,40},{28,44},{32,4... | collective-permute-start | bytes 6291464 | tf_op jit(solution)/shard_map/ppermute | solution.py:14
  486.1 29.2 %copy-start.6 = (bf16[4,128,2048]{2,1,0:T(8,128)(2,1)S(1)}, bf16[4,128,2048]{2,1,0:T(8,128)(2,1)}, u32[]{:S(2)}) copy-start(bf16[4,128,2048]{2,1,0:T(8,128)(2,1)} %param.24) | copy-start | bytes 6291460
  522.1 3.4 copy-start.5
  526.1 16.7 %copy-start = (bf16[16,8,128,128]{3,2,0,1:T(8,128)(2,1)}, bf16[16,8,128,128]{3,2,0,1:T(8,128)(2,1)S(1)}, u32[]{:S(2)}) copy-start(bf16[16,8,128,128]{3,2,0,1:T(8,128)(2,1)S(1)} %select_bitcast_fusion) | copy-start | bytes 12582916
  715.7 555.8 %collective-permute-start.7 = (f32[4,128,2048]{2,1,0:T(8,128)}, f32[4,128,2048]{2,1,0:T(8,128)}, u32[]{:S(2)}, u32[]{:S(2)}) collective-permute-start(f32[4,128,2048]{2,1,0:T(8,128)} %get-tuple-element.127), channel_id=1, source_target_pairs={{16,0},{20,4},{24,8},{28,12},{32,16},{36,20},{40,24},{44,28},{48,3... | collective-permute-start | bytes 12582920 | tf_op jit(solution)/shard_map/ppermute | solution.py:14
  725.6 545.8 %collective-permute-start.6 = (f32[4,128,2048]{2,1,0:T(8,128)}, f32[4,128,2048]{2,1,0:T(8,128)}, u32[]{:S(2)}, u32[]{:S(2)}) collective-permute-start(f32[4,128,2048]{2,1,0:T(8,128)} %get-tuple-element.128), channel_id=1, source_target_pairs={{12,0},{16,4},{20,8},{24,12},{28,16},{32,20},{36,24},{40,28},{44,3... | collective-permute-start | bytes 12582920 | tf_op jit(solution)/shard_map/ppermute | solution.py:14
  730.0 541.4 %collective-permute-start.5 = (f32[4,128,2048]{2,1,0:T(8,128)}, f32[4,128,2048]{2,1,0:T(8,128)}, u32[]{:S(2)}, u32[]{:S(2)}) collective-permute-start(f32[4,128,2048]{2,1,0:T(8,128)} %get-tuple-element.129), channel_id=1, source_target_pairs={{8,0},{12,4},{16,8},{20,12},{24,16},{28,20},{32,24},{36,28},{40,32... | collective-permute-start | bytes 12582920 | tf_op jit(solution)/shard_map/ppermute | solution.py:14
  734.5 536.9 %collective-permute-start.4 = (f32[4,128,2048]{2,1,0:T(8,128)}, f32[4,128,2048]{2,1,0:T(8,128)}, u32[]{:S(2)}, u32[]{:S(2)}) collective-permute-start(f32[4,128,2048]{2,1,0:T(8,128)} %get-tuple-element.126), channel_id=1, source_target_pairs={{4,0},{8,4},{12,8},{16,12},{20,16},{24,20},{28,24},{32,28},{36,32}... | collective-permute-start | bytes 12582920 | tf_op jit(solution)/shard_map/ppermute | solution.py:14
  772.8 4.5 copy-start.2
  783.0 4.5 copy-start.3
  793.2 4.5 copy-start.4
  1005.2 15.8 %copy-start.1 = (bf16[4,128,2048]{1,2,0:T(8,128)(2,1)S(1)}, bf16[4,128,2048]{1,2,0:T(8,128)(2,1)}, u32[]{:S(2)}) copy-start(bf16[4,128,2048]{1,2,0:T(8,128)(2,1)} %copy.160) | copy-start | bytes 6291460
Sparse Core Ops, SparseCore 0:
  1021.1 248.8 all-reduce.10
where the time goes:
time: 1300 us; the launch traced here: 1290 us
  local copies, waits for them, and re-layouts  807 us (62%)
  waiting for transfers between devices  241 us (19%)
  other arithmetic  126 us (10%)
  matrix products  78 us (6%)
  starting transfers between devices  22.1 us (2%)
  between operations  15.1 us (1%)
    gather x2, local copies, waits for them, and re-layouts, filter_blocks(): jnp.take(narrow, jnp.clip(lag_offsets, 0, filters.shape[1] - 1), axis=1)  483 us
    psum x1, waiting for transfers between devices, per_device(): filter_grad = lax.psum(local_filters, ('ctx', 'ch')) * norm_factor  241 us
    scatter-add x8, other arithmetic, per_device(): partial_value.at[back_rows[:, lag_index]]  69.9 us
    rev x8, local copies, waits for them, and re-layouts, lag_sums(): flipped = square[:, :, ::-1]  54.3 us
    reshape x8, local copies, waits for them, and re-layouts, lag_sums(): skewed.reshape(filter_count, side_length, 2 * side_length - 1)  49.4 us
    reshape x8, local copies, waits for them, and re-layouts, per_device(): adjoint_term.reshape(slot_count, tile_rows, channels)  43.4 us
    dot_general x8, matrix products, per_device(): jnp.einsum('fij,sjrfc->sirfc', blocks[:, lag_index], shaped, preferred_el...  42.7 us
    slice x9, local copies, waits for them, and re-layouts, per_device(): selected[:, lag_index]  37.9 us
  transfers between devices with their start and end apart: 9, of which 1 were waited for; matrix products, arithmetic and copies ran while one was open for 78% of the time, Pallas kernels for 0%

commit v1 on v0

--- a/solution.py
+++ b/solution.py
@@ -104,7 +104,7 @@
         total_tiles * tile_rows * channels * lax.axis_size("ch") / filter_count
     )
     local_filters = spread_lags(jnp.stack(squares), lag_count)
-    filter_grad = lax.psum(local_filters, ("ctx", "ch")) * norm_factor
+    filter_grad = lax.psum(lax.psum(local_filters, "ctx"), "ch") * norm_factor
     row_count = (farthest + 1) * slot_count
     partial_value = jnp.zeros((row_count, tile_rows, channels), jnp.float32)
     back_rows = jnp.clip((myself - holder) * slot_count + within, 0, row_count - 1)

time: 1300 us -> 1260 us (0.969)
  waiting for transfers between devices: 241 us -> 187 us
  local copies, waits for them, and re-layouts: 807 us -> 821 us
    psum x1 -> x2, waiting for transfers between devices: 241 us -> 187 us  [per_device(): filter_grad = lax.psum(lax.psum(local_filters, 'ctx'), 'ch') * norm_factor]
    rev x8, local copies, waits for them, and re-layouts: 54.3 us -> 68.2 us  [lag_sums(): flipped = square[:, :, ::-1]]
    unnamed x32 -> x44, local copies, waits for them, and re-layouts: 33.9 us -> 34 us
  transfers between devices with their start and end apart: 9 -> 10, of which waited for: 1 -> 2; matrix products, arithmetic and copies ran while one was open for 78% -> 81% of each run, Pallas kernels for 0% -> 0%
where the time goes in v1:
time: 1260 us; the launch traced here: 1250 us
  local copies, waits for them, and re-layouts  821 us (65%)
  waiting for transfers between devices  187 us (15%)
  other arithmetic  126 us (10%)
  matrix products  74.6 us (6%)
  starting transfers between devices  22.4 us (2%)
  between operations  15.1 us (1%)
    gather x2, local copies, waits for them, and re-layouts, filter_blocks(): jnp.take(narrow, jnp.clip(lag_offsets, 0, filters.shape[1] - 1), axis=1)  483 us
    psum x2, waiting for transfers between devices, per_device(): filter_grad = lax.psum(lax.psum(local_filters, 'ctx'), 'ch') * norm_factor  187 us
    scatter-add x8, other arithmetic, per_device(): partial_value.at[back_rows[:, lag_index]]  69.9 us
    rev x8, local copies, waits for them, and re-layouts, lag_sums(): flipped = square[:, :, ::-1]  68.2 us
    reshape x8, local copies, waits for them, and re-layouts, lag_sums(): skewed.reshape(filter_count, side_length, 2 * side_length - 1)  49.4 us
    reshape x8, local copies, waits for them, and re-layouts, per_device(): adjoint_term.reshape(slot_count, tile_rows, channels)  43.4 us
    slice x9, local copies, waits for them, and re-layouts, per_device(): selected[:, lag_index]  37.5 us
    select_n x8, local copies, waits for them, and re-layouts, per_device(): jnp.where(present[:, lag_index, None, None, None, None], adjoint_term, 0.0)  34.8 us
  transfers between devices with their start and end apart: 10, of which 2 were waited for; matrix products, arithmetic and copies ran while one was open for 81% of the time, Pallas kernels for 0%

profile of v1, /device:TPU:1, one launch (start us, length us, event | category | flops | bytes accessed | tf_op | source)
XLA Modules:
  0.0 1245.5 jit_solution(14663723464845822097)
XLA Ops:
  32.2 454.0 %gather_fusion.4 = bf16[131072,16]{1,0:T(8,128)(2,1)} fusion(bf16[16,1024]{0,1:T(8,128)(2,1)S(1)} %copy.164, s32[131072]{0:T(1024)S(1)} %broadcast_clamp_fusion), kind=kCustom, calls=%fused_computation.4 | custom fusion | bytes 8912896 | tf_op jit(solution)/shard_map/jit(_take)/gather | solution.py:25
  486.1 29.2 %copy.166 = bf16[8,128,128,16]{2,1,3,0:T(8,128)(2,1)} copy(bf16[8,128,128,16]{3,2,1,0:T(8,128)(2,1)} %bitcast.207) | data formatting | bytes 8388608 | tf_op jit(solution)/shard_map/jit(_take)/gather | solution.py:25
  547.7 5.4 copy.186
  553.1 4.7 copy.188
  557.7 5.4 copy.189
  563.1 4.7 copy.191
  567.8 5.4 copy.192
  573.2 4.7 copy.194
  577.8 5.4 copy.195
  583.2 4.7 copy.197
  587.9 5.4 copy.198
  593.3 4.7 copy.200
  598.0 5.6 copy.201
  608.2 5.4 copy.204
  618.2 5.4 copy.207
  623.9 9.7 broadcast_in_dim.155
  633.6 9.0 scatter_fusion
  642.5 9.0 scatter_fusion.1
  651.6 9.0 scatter_fusion.2
  660.6 9.0 scatter_fusion.3
  669.6 8.7 scatter_fusion.4
  678.2 8.6 scatter_fusion.5
  686.9 8.3 scatter_fusion.6
  695.1 8.3 scatter_fusion.7
  703.4 12.2 fusion.52
  742.8 11.4 gather_fusion.3
  754.2 8.7 select_select_fusion
  762.9 5.9 fusion.53
  815.3 9.5 rev.24
  829.0 6.2 reshape.668
  840.9 9.2 rev.25
  854.3 6.2 reshape.670
  865.5 9.7 rev.26
  879.3 6.2 reshape.672
  890.6 9.2 rev.27
  904.0 6.2 reshape.674
  915.2 9.4 rev.28
  928.8 6.2 reshape.676
  936.7 9.3 rev.29
  950.2 6.2 reshape.678
  958.1 6.0 rev.30
  968.3 6.2 reshape.680
  978.5 5.8 rev.31
  988.5 6.3 reshape.682
  1019.2 10.3 add_bitcast_fusion
  1031.8 151.5 %all-reduce.12.cloned.1.call-done = f32[16,1024]{1,0:T(8,128)} async-done(((f32[16,1024]{1,0:T(8,128)}), f32[16,1024]{1,0:T(8,128)}) %all-reduce.12.cloned.1.call-update) | async-done | bytes 65552 | tf_op jit(solution)/shard_map/psum | solution.py:107
  1191.1 35.2 %all-reduce.14.cloned.1.call-done = f32[16,1024]{1,0:T(8,128)} async-done(((f32[16,1024]{1,0:T(8,128)}), f32[16,1024]{1,0:T(8,128)}) %all-reduce.14.cloned.1.call-update) | async-done | bytes 65552 | tf_op jit(solution)/shard_map/psum | solution.py:107
  1227.8 10.4 fusion.5
  (189 shorter events, 237.8 us)
Async XLA Ops:
  7.2 24.7 %copy-start.13 = (f32[16,1024]{1,0:T(8,128)S(1)}, f32[16,1024]{1,0:T(8,128)}, u32[]{:S(2)}) copy-start(f32[16,1024]{1,0:T(8,128)} %param.25) | copy-start | bytes 196612
  7.2 1176.1 %all-reduce.12.cloned.1.call-start = ((), (), s32[]{:S(2)}) async-start(), calls=%async_computation | async-start | bytes 131072 | tf_op jit(solution)/shard_map/psum | solution.py:107
  7.2 718.4 %collective-permute-start = (bf16[4,128,2048]{2,1,0:T(8,128)(2,1)}, bf16[4,128,2048]{2,1,0:T(8,128)(2,1)}, u32[]{:S(2)}, u32[]{:S(2)}) collective-permute-start(bf16[4,128,2048]{2,1,0:T(8,128)(2,1)} %param.22), channel_id=1, source_target_pairs={{0,4},{4,8},{8,12},{12,16},{16,20},{20,24},{24,28},{28,32},{32,36}... | collective-permute-start | bytes 6291464 | tf_op jit(solution)/shard_map/ppermute | solution.py:14
  11.8 718.2 %collective-permute-start.1 = (bf16[4,128,2048]{2,1,0:T(8,128)(2,1)}, bf16[4,128,2048]{2,1,0:T(8,128)(2,1)}, u32[]{:S(2)}, u32[]{:S(2)}) collective-permute-start(bf16[4,128,2048]{2,1,0:T(8,128)(2,1)} %param.22), channel_id=1, source_target_pairs={{0,8},{4,12},{8,16},{12,20},{16,24},{20,28},{24,32},{28,36},{32,40... | collective-permute-start | bytes 6291464 | tf_op jit(solution)/shard_map/ppermute | solution.py:14
  16.3 718.2 %collective-permute-start.2 = (bf16[4,128,2048]{2,1,0:T(8,128)(2,1)}, bf16[4,128,2048]{2,1,0:T(8,128)(2,1)}, u32[]{:S(2)}, u32[]{:S(2)}) collective-permute-start(bf16[4,128,2048]{2,1,0:T(8,128)(2,1)} %param.22), channel_id=1, source_target_pairs={{0,12},{4,16},{8,20},{12,24},{16,28},{20,32},{24,36},{28,40},{32,4... | collective-permute-start | bytes 6291464 | tf_op jit(solution)/shard_map/ppermute | solution.py:14
  19.9 719.7 %collective-permute-start.3 = (bf16[4,128,2048]{2,1,0:T(8,128)(2,1)}, bf16[4,128,2048]{2,1,0:T(8,128)(2,1)}, u32[]{:S(2)}, u32[]{:S(2)}) collective-permute-start(bf16[4,128,2048]{2,1,0:T(8,128)(2,1)} %param.22), channel_id=1, source_target_pairs={{0,16},{4,20},{8,24},{12,28},{16,32},{20,36},{24,40},{28,44},{32,4... | collective-permute-start | bytes 6291464 | tf_op jit(solution)/shard_map/ppermute | solution.py:14
  486.1 29.2 %copy-start.12 = (bf16[4,128,2048]{2,1,0:T(8,128)(2,1)S(1)}, bf16[4,128,2048]{2,1,0:T(8,128)(2,1)}, u32[]{:S(2)}) copy-start(bf16[4,128,2048]{2,1,0:T(8,128)(2,1)} %param.24) | copy-start | bytes 6291460
  522.1 3.4 copy-start.11
  526.1 16.7 %copy-start = (bf16[16,8,128,128]{3,2,0,1:T(8,128)(2,1)}, bf16[16,8,128,128]{3,2,0,1:T(8,128)(2,1)S(1)}, u32[]{:S(2)}) copy-start(bf16[16,8,128,128]{3,2,0,1:T(8,128)(2,1)S(1)} %select_bitcast_fusion) | copy-start | bytes 12582916
  715.7 512.1 %collective-permute-start.7 = (f32[4,128,2048]{2,1,0:T(8,128)}, f32[4,128,2048]{2,1,0:T(8,128)}, u32[]{:S(2)}, u32[]{:S(2)}) collective-permute-start(f32[4,128,2048]{2,1,0:T(8,128)} %get-tuple-element.127), channel_id=1, source_target_pairs={{16,0},{20,4},{24,8},{28,12},{32,16},{36,20},{40,24},{44,28},{48,3... | collective-permute-start | bytes 12582920 | tf_op jit(solution)/shard_map/ppermute | solution.py:14
  725.6 502.2 %collective-permute-start.6 = (f32[4,128,2048]{2,1,0:T(8,128)}, f32[4,128,2048]{2,1,0:T(8,128)}, u32[]{:S(2)}, u32[]{:S(2)}) collective-permute-start(f32[4,128,2048]{2,1,0:T(8,128)} %get-tuple-element.128), channel_id=1, source_target_pairs={{12,0},{16,4},{20,8},{24,12},{28,16},{32,20},{36,24},{40,28},{44,3... | collective-permute-start | bytes 12582920 | tf_op jit(solution)/shard_map/ppermute | solution.py:14
  730.1 497.7 %collective-permute-start.5 = (f32[4,128,2048]{2,1,0:T(8,128)}, f32[4,128,2048]{2,1,0:T(8,128)}, u32[]{:S(2)}, u32[]{:S(2)}) collective-permute-start(f32[4,128,2048]{2,1,0:T(8,128)} %get-tuple-element.129), channel_id=1, source_target_pairs={{8,0},{12,4},{16,8},{20,12},{24,16},{28,20},{32,24},{36,28},{40,32... | collective-permute-start | bytes 12582920 | tf_op jit(solution)/shard_map/ppermute | solution.py:14
  734.6 493.3 %collective-permute-start.4 = (f32[4,128,2048]{2,1,0:T(8,128)}, f32[4,128,2048]{2,1,0:T(8,128)}, u32[]{:S(2)}, u32[]{:S(2)}) collective-permute-start(f32[4,128,2048]{2,1,0:T(8,128)} %get-tuple-element.126), channel_id=1, source_target_pairs={{4,0},{8,4},{12,8},{16,12},{20,16},{24,20},{28,24},{32,28},{36,32}... | collective-permute-start | bytes 12582920 | tf_op jit(solution)/shard_map/ppermute | solution.py:14
  772.8 4.5 copy-start.9
  783.0 4.5 copy-start.10
  988.5 16.1 %copy-start.4 = (bf16[4,1,128,2048]{2,3,0,1:T(8,128)(2,1)S(1)}, bf16[4,1,128,2048]{2,3,0,1:T(8,128)(2,1)}, u32[]{:S(2)}) copy-start(bf16[4,1,128,2048]{2,3,0,1:T(8,128)(2,1)} %copy.174) | copy-start | bytes 6291460
  1004.3 222.0 %all-reduce.14.cloned.1.call-start = ((), (), s32[]{:S(2)}) async-start(), calls=%async_computation.1 | async-start | bytes 131072 | tf_op jit(solution)/shard_map/psum | solution.py:107
  1004.6 3.9 copy-start.1
  1004.6 3.9 copy-start.5
  1008.5 2.8 copy-start.6
  1011.2 2.7 copy-start.7
  1013.9 2.6 copy-start.8
  1016.5 2.7 copy-start.2
  1029.5 153.7 %copy-start.3 = (bf16[4,128,2048]{1,2,0:T(8,128)(2,1)S(1)}, bf16[4,128,2048]{1,2,0:T(8,128)(2,1)}, u32[]{:S(2)}) copy-start(bf16[4,128,2048]{1,2,0:T(8,128)(2,1)} %copy.160) | copy-start | bytes 6291460
Sparse Core Ops, SparseCore 0:
  1004.4 178.7 all-reduce.11
  1185.5 40.7 all-reduce.13
